TPU v7x, 32 devices: a whole 2x2x4 slice. The times are simulated.
32 devices in a mesh: curve: 8 (over z, y), band: 4 (over x, core).
Axes of the slice: x: 2, y: 2, z: 4, core: 2. Of those that a mesh axis runs over, the one named last changes fastest.
Arguments:
- state: float32 [16, 2048, 128], P('band', 'curve'), may hold values from -3 to 3
- blocks: bfloat16 [2048, 4, 128, 128], P('curve', 'band'), may hold values from -0.25 to 0.25
- diag_blocks: bfloat16 [2048, 128, 128], P(('curve', 'band')), may hold values from -1 to 1, as said below
- block_cols: int32 [2048, 4], P('curve', 'band'), may hold values from 0 to 2047, as said below
Outputs:
- updated: float32 [16, 2048, 128], P('band', 'curve')
Inputs may be any that keep to these rules, and one draw needn't show every extreme that they name: `diag_blocks`: every diagonal block is symmetric. `block_cols`: A column is never the row's own patch, and no pair of patches is stored twice, in either order. The owner of patch p is index p // 256 of curve. Of the 256 rows of one index of curve, in each slot exactly 8 have their column on another index: 2 on each of 4 other indices; the columns of the others lie on the own index.
All inputs are finite; a program needn't handle non-finite values.
Results may differ from a plain program's by a relative error of at most 0.0003.
The roundings to bfloat16 on the way count: a program that leaves them out, or rounds other values in their place, can miss the bound.
Values may be sent and summed in bfloat16 or wider, within the bound.
No kernel may reach another device: no remote copies, remote signals or barrier semaphores. Data moves between devices by JAX's collectives and lax.ppermute only.
A program may use at most 64 MiB of HBM per device.

v0:
```python
import jax
import jax.numpy as jnp
from jax import lax
from jax.sharding import PartitionSpec as P

CAP = 2
TAYLOR = 16
epsilon = 1e-06
time_step = 0.5
quadratic = 1.0


def nonlinear(field):
    return quadratic * field * field - field * field * field


def phi_weights(alpha_first, beta_first, alpha_second):

    def advance(turn, carry):
        term_one, term_two, total_one, total_two = carry
        factor = time_step / (turn + 1.0)
        next_one = factor * (alpha_first * term_one + beta_first * term_two)
        next_two = factor * (beta_first * term_one + alpha_second * term_two)
        return (next_one, next_two, total_one + next_one, total_two + next_two)

    ones = jnp.ones_like(alpha_first)
    zeros = jnp.zeros_like(alpha_first)
    result = lax.fori_loop(1, TAYLOR, advance, (ones, zeros, ones, zeros))
    return (result[2], result[3])


def routing(block_cols):
    groups = lax.axis_size("curve")
    here = lax.axis_index("curve")
    patch_rows = block_cols.shape[0]
    columns = block_cols[:, 0]
    owner = columns // patch_rows
    target = columns % patch_rows
    remote = owner != here
    peers = jnp.arange(groups, dtype=jnp.int32)
    member = ((owner[:, None] == peers[None, :]) & remote[:, None]).astype(jnp.int32)
    rank = jnp.sum(jnp.cumsum(member, axis=0) * member, axis=1) - 1
    bucket = jnp.where(remote, owner * CAP + rank, groups * CAP)
    pick = jnp.where(remote, patch_rows + owner * CAP + rank, target)
    wanted = jnp.full((groups * CAP + 1,), -1, jnp.int32).at[bucket].set(target)
    asked = lax.all_to_all(
        wanted[:-1].reshape(groups, CAP), "curve", split_axis=0, concat_axis=0, tiled=True
    )
    asked_flat = asked.reshape(-1)
    return (remote, target, bucket, pick, jnp.maximum(asked_flat, 0), asked_flat >= 0)


def local_product(whole, blocks, diag_blocks, plan):
    remote, target, bucket, pick, asked_index, asked_valid = plan
    groups = lax.axis_size("curve")
    vectors, patch_rows, node_count = whole.shape
    reply = whole[:, asked_index, :].reshape(vectors, groups, CAP, node_count)
    arrived = lax.all_to_all(reply, "curve", split_axis=1, concat_axis=1, tiled=True)
    pool = jnp.concatenate([whole, arrived.reshape(vectors, groups * CAP, node_count)], axis=1)
    gathered = pool[:, pick, :]
    stored = blocks[:, 0]
    result = jnp.einsum("rac,vrc->vra", stored, gathered, preferred_element_type=jnp.float32)
    mirrored = jnp.einsum("rac,vra->vrc", stored, whole, preferred_element_type=jnp.float32)
    kept = jnp.where(remote[None, :, None], 0.0, mirrored)
    result = result.at[:, target, :].add(kept)
    outgoing = (
        jnp.zeros((vectors, groups * CAP + 1, node_count), jnp.float32)
        .at[:, bucket, :]
        .add(mirrored)
    )
    outgoing = outgoing[:, :-1, :].reshape(vectors, groups, CAP, node_count)
    returned = lax.all_to_all(outgoing, "curve", split_axis=1, concat_axis=1, tiled=True)
    returned = jnp.where(
        asked_valid[None, :, None], returned.reshape(vectors, groups * CAP, node_count), 0.0
    )
    result = result.at[:, asked_index, :].add(returned)
    quarter = diag_blocks.shape[0]
    start = lax.axis_index("band") * quarter
    own_rows = lax.dynamic_slice_in_dim(whole, start, quarter, 1)
    diagonal = jnp.einsum("rac,vrc->vra", diag_blocks, own_rows, preferred_element_type=jnp.float32)
    current = lax.dynamic_slice_in_dim(result, start, quarter, 1)
    return lax.dynamic_update_slice_in_dim(result, current + diagonal, start, 1)


def operate(vector, blocks, diag_blocks, plan):
    whole = lax.all_gather(vector, "band", axis=0, tiled=True)
    product = lax.psum_scatter(
        local_product(whole, blocks, diag_blocks, plan), "band", scatter_dimension=0, tiled=True
    )
    return product


def body(state, blocks, diag_blocks, block_cols):
    plan = routing(block_cols)
    drive = operate(state.astype(jnp.bfloat16), blocks, diag_blocks, plan) + nonlinear(state)
    drive_norm = lax.psum(jnp.sum(drive * drive, axis=(1, 2)), "curve")
    beta_zero = jnp.sqrt(drive_norm + epsilon)
    first = drive / beta_zero[:, None, None]
    image = operate(first.astype(jnp.bfloat16), blocks, diag_blocks, plan)
    alpha_first, energy = lax.psum(
        (jnp.sum(first * image, axis=(1, 2)), jnp.sum(image * image, axis=(1, 2))), "curve"
    )
    rest = image - alpha_first[:, None, None] * first
    beta_first = jnp.sqrt(jnp.maximum(energy - alpha_first * alpha_first, 0.0) + epsilon)
    second = rest / beta_first[:, None, None]
    image_second = operate(second.astype(jnp.bfloat16), blocks, diag_blocks, plan)
    image_second = image_second - beta_first[:, None, None] * first
    alpha_second = lax.psum(jnp.sum(second * image_second, axis=(1, 2)), "curve")
    weight_one, weight_two = phi_weights(alpha_first, beta_first, alpha_second)
    combined = weight_one[:, None, None] * first + weight_two[:, None, None] * second
    updated = state + time_step * beta_zero[:, None, None] * combined
    return updated


def solution(mesh):
    return jax.shard_map(
        body,
        mesh=mesh,
        in_specs=(
            P("band", "curve", None),
            P("curve", "band", None, None),
            P(("curve", "band"), None, None),
            P("curve", "band"),
        ),
        out_specs=P("band", "curve", None),
        check_vma=False,
    )
```

profile of v0, /device:TPU:0, one launch (start us, length us, event | category | flops | bytes accessed | tf_op | source)
XLA Modules:
  0.0 534.8 jit_solution(13686195170682434651)
XLA Ops:
  6.5 1.9 convert_element_type.21
  8.5 0.7 compare_select_fusion
  9.2 0.7 fusion.44
  10.8 0.7 and_select_fusion.3
  11.5 1.4 scatter_custom_fusion
  12.9 0.7 all_to_all.24
  13.6 7.3 %all-to-all-start = ((s32[8,1,2]{2,1,0:T(1,128)}), s32[8,1,2]{2,1,0:T(1,128)S(1)}, u32[]{:S(2)}, u32[]{:S(2)}) async-start(s32[8,1,2]{2,1,0:T(1,128)} %bitcast.7), calls=%async_computation | async-start | bytes 8192 | tf_op jit(solution)/shard_map/all_to_all | solution.py:46
  20.9 0.7 fusion.43
  21.6 5.8 %all-to-all-done = s32[8,1,2]{2,1,0:T(1,128)S(1)} async-done(((s32[8,1,2]{2,1,0:T(1,128)}), s32[8,1,2]{2,1,0:T(1,128)S(1)}, u32[]{:S(2)}, u32[]{:S(2)}) %all-to-all-start) | async-done | bytes 96 | tf_op jit(solution)/shard_map/all_to_all | solution.py:46
  27.7 0.7 all-gather.4.cloned.1.call-done
  28.3 1.9 copy.32
  30.3 1.2 gather_fusion
  31.4 5.5 %all-to-all-start.1 = ((bf16[16,8,2,128]{3,0,2,1:T(8,128)(2,1)}), bf16[16,8,2,128]{3,0,2,1:T(8,128)(2,1)S(1)}, u32[]{:S(2)}, u32[]{:S(2)}) async-start(bf16[16,8,2,128]{3,0,2,1:T(8,128)(2,1)} %bitcast.9), calls=%async_computation.1 | async-start | bytes 131072 | tf_op jit(solution)/shard_map/all_to_all | solution.py:58
  37.0 8.0 %broadcast_select_fusion.6 = (f32[256,16,128]{2,1,0:T(8,128)}, f32[256,16,128]{2,1,0:T(8,128)}) fusion(pred[256]{0:T(512)(128)(4,1)S(1)} %fusion.43, bf16[256,1,128,128]{3,2,1,0:T(8,128)(2,1)} %param.7, bf16[16,256,128]{2,1,0:T(8,128)(2,1)} %all-gather.4.cloned.1.call-done), kind=kOutput, calls=%fused_computation.56 | convolution fusion | flops 134742016 | bytes 13631744 | tf_op jit(solution)/shard_map/rac,vra->vrc/dot_general | solution.py:63
  45.0 20.9 %scatter_fusion.1 = f32[16,17,128]{2,0,1:T(8,128)S(1)} fusion(f32[16,17,128]{2,0,1:T(8,128)S(1)} %broadcast.192.clone, s32[256]{0:T(256)S(1)} %bitcast.116, f32[256,16,128]{2,1,0:T(8,128)} %get-tuple-element.211), kind=kCustom, calls=%fused_computation.8 | custom fusion | flops 524288 | bytes 6292480 | tf_op jit(solution)/shard_map/scatter-add | solution.py:69
  66.6 6.0 %all-to-all-start.2 = ((f32[16,8,2,128]{3,0,2,1:T(8,128)}), f32[16,8,2,128]{3,0,2,1:T(8,128)S(1)}, u32[]{:S(2)}, u32[]{:S(2)}) async-start(f32[16,8,2,128]{3,0,2,1:T(8,128)} %bitcast.16), calls=%async_computation.2 | async-start | bytes 262144 | tf_op jit(solution)/shard_map/all_to_all | solution.py:72
  72.6 1.1 pad_maximum_fusion
  73.7 3.0 gather_fusion.1
  76.7 9.5 %fusion.14 = f32[16,256,128]{2,0,1:T(8,128)} fusion(bf16[256,1,128,128]{3,2,1,0:T(8,128)(2,1)} %param.7, bf16[256,16,128]{2,1,0:T(8,128)(2,1)} %gather_fusion.1), kind=kOutput, calls=%fused_computation.36 | convolution fusion | flops 134217728 | bytes 11534336 | tf_op jit(solution)/shard_map/rac,vrc->vra/dot_general | solution.py:62
  86.2 31.4 %scatter_fusion = f32[16,256,128]{2,0,1:T(8,128)} fusion(f32[16,256,128]{2,0,1:T(8,128)} %fusion.14, s32[256]{0:T(256)S(1)} %bitcast.112, f32[256,16,128]{2,1,0:T(8,128)} %get-tuple-element.210), kind=kCustom, calls=%fused_computation.7 | custom fusion | flops 524288 | bytes 6292480 | tf_op jit(solution)/shard_map/scatter-add | solution.py:65
  117.7 2.5 scatter_fusion.2
  120.3 3.0 fusion.24
  123.3 3.6 copy.35
  127.0 31.7 %reduce-scatter.4.cloned.1.call-done = f32[4,256,128]{2,1,0:T(8,128)} async-done(((f32[16,256,128]{2,1,0:T(8,128)}), f32[4,256,128]{2,1,0:T(8,128)}) %reduce-scatter.4.cloned.1.call-update) | async-done | bytes 524304 | tf_op jit(solution)/shard_map/reduce_scatter | solution.py:87
  158.8 1.3 multiply_reduce_fusion.3
  160.0 21.3 %psum.28 = f32[4]{0:T(128)S(1)} all-reduce(f32[4]{0:T(128)S(1)} %multiply_reduce_fusion.3), channel_id=1, replica_groups=mesh['curve'=8,'band'=4] {'curve'}, use_global_device_ids=true, to_apply=%region_9.10 | all-reduce | flops 4 | bytes 32 | tf_op jit(solution)/shard_map/psum | solution.py:96
  181.4 1.9 fusion.51
  183.3 13.2 %all-gather.6.cloned.1.call-done = bf16[16,256,128]{2,1,0:T(8,128)(2,1)} async-done(((bf16[4,256,128]{2,1,0:T(8,128)(2,1)}), bf16[16,256,128]{2,1,0:T(8,128)(2,1)}) %all-gather.6.cloned.1.call-update) | async-done | bytes 1048592 | tf_op jit(solution)/shard_map/all_gather | solution.py:86
  196.5 2.9 copy.37
  199.3 2.4 gather_fusion.2
  201.7 5.5 %all-to-all-start.3 = ((bf16[16,8,2,128]{3,0,2,1:T(8,128)(2,1)}), bf16[16,8,2,128]{3,0,2,1:T(8,128)(2,1)S(1)}, u32[]{:S(2)}, u32[]{:S(2)}) async-start(bf16[16,8,2,128]{3,0,2,1:T(8,128)(2,1)} %bitcast.21), calls=%async_computation.4 | async-start | bytes 131072 | tf_op jit(solution)/shard_map/all_to_all | solution.py:58
  207.3 8.0 %broadcast_select_fusion.5 = (f32[256,16,128]{2,1,0:T(8,128)}, f32[256,16,128]{2,1,0:T(8,128)}) fusion(pred[256]{0:T(512)(128)(4,1)S(1)} %fusion.43, bf16[256,1,128,128]{3,2,1,0:T(8,128)(2,1)} %param.7, bf16[16,256,128]{2,1,0:T(8,128)(2,1)} %all-gather.6.cloned.1.call-done), kind=kOutput, calls=%fused_computation.55 | convolution fusion | flops 134742016 | bytes 13631744 | tf_op jit(solution)/shard_map/rac,vra->vrc/dot_general | solution.py:63
  215.3 20.9 %scatter_fusion.4 = f32[16,17,128]{2,0,1:T(8,128)S(1)} fusion(f32[16,17,128]{2,0,1:T(8,128)S(1)} %broadcast.192.clone.1, s32[256]{0:T(256)S(1)} %bitcast.117, f32[256,16,128]{2,1,0:T(8,128)} %get-tuple-element.213), kind=kCustom, calls=%fused_computation.11 | custom fusion | flops 524288 | bytes 6292480 | tf_op jit(solution)/shard_map/scatter-add | solution.py:69
  236.9 6.0 %all-to-all-start.4 = ((f32[16,8,2,128]{3,0,2,1:T(8,128)}), f32[16,8,2,128]{3,0,2,1:T(8,128)S(1)}, u32[]{:S(2)}, u32[]{:S(2)}) async-start(f32[16,8,2,128]{3,0,2,1:T(8,128)} %bitcast.25), calls=%async_computation.5 | async-start | bytes 262144 | tf_op jit(solution)/shard_map/all_to_all | solution.py:72
  242.9 2.3 pad_maximum_fusion.1
  245.3 3.0 gather_fusion.3
  248.3 9.5 %fusion.17 = f32[16,256,128]{2,0,1:T(8,128)} fusion(bf16[256,1,128,128]{3,2,1,0:T(8,128)(2,1)} %param.7, bf16[256,16,128]{2,1,0:T(8,128)(2,1)} %gather_fusion.3), kind=kOutput, calls=%fused_computation.37 | convolution fusion | flops 134217728 | bytes 11534336 | tf_op jit(solution)/shard_map/rac,vrc->vra/dot_general | solution.py:62
  257.8 31.4 %scatter_fusion.3 = f32[16,256,128]{2,0,1:T(8,128)} fusion(f32[16,256,128]{2,0,1:T(8,128)} %fusion.17, s32[256]{0:T(256)S(1)} %bitcast.113, f32[256,16,128]{2,1,0:T(8,128)} %get-tuple-element.212), kind=kCustom, calls=%fused_computation.10 | custom fusion | flops 524288 | bytes 6292480 | tf_op jit(solution)/shard_map/scatter-add | solution.py:65
  289.3 2.5 scatter_fusion.5
  291.8 3.1 fusion.26
  295.0 3.6 copy.40
  298.7 31.7 %reduce-scatter.6.cloned.1.call-done = f32[4,256,128]{2,1,0:T(8,128)} async-done(((f32[16,256,128]{2,1,0:T(8,128)}), f32[4,256,128]{2,1,0:T(8,128)}) %reduce-scatter.6.cloned.1.call-update) | async-done | bytes 524304 | tf_op jit(solution)/shard_map/reduce_scatter | solution.py:87
  330.4 1.2 multiply_reduce_fusion.1
  331.6 21.3 %all-reduce = (f32[4]{0:T(128)S(1)}, f32[4]{0:T(128)S(1)}) all-reduce(f32[4]{0:T(128)S(1)} %get-tuple-element.175, f32[4]{0:T(128)S(1)} %get-tuple-element.174), channel_id=1, replica_groups=mesh['curve'=8,'band'=4] {'curve'}, use_global_device_ids=true, to_apply=%region_15.16 | all-reduce | flops 8 | bytes 64 | tf_op jit(solution)/shard_map/psum | solution.py:100
  353.0 1.9 fusion.50
  354.9 13.2 %all-gather.8.cloned.1.call-done = bf16[16,256,128]{2,1,0:T(8,128)(2,1)} async-done(((bf16[4,256,128]{2,1,0:T(8,128)(2,1)}), bf16[16,256,128]{2,1,0:T(8,128)(2,1)}) %all-gather.8.cloned.1.call-update) | async-done | bytes 1048592 | tf_op jit(solution)/shard_map/all_gather | solution.py:86
  368.1 2.9 copy.42
  370.9 2.4 gather_fusion.4
  373.4 5.5 %all-to-all-start.5 = ((bf16[16,8,2,128]{3,0,2,1:T(8,128)(2,1)}), bf16[16,8,2,128]{3,0,2,1:T(8,128)(2,1)S(1)}, u32[]{:S(2)}, u32[]{:S(2)}) async-start(bf16[16,8,2,128]{3,0,2,1:T(8,128)(2,1)} %bitcast.30), calls=%async_computation.7 | async-start | bytes 131072 | tf_op jit(solution)/shard_map/all_to_all | solution.py:58
  378.9 8.0 %broadcast_select_fusion.4 = (f32[256,16,128]{2,1,0:T(8,128)}, f32[256,16,128]{2,1,0:T(8,128)}) fusion(pred[256]{0:T(512)(128)(4,1)S(1)} %fusion.43, bf16[256,1,128,128]{3,2,1,0:T(8,128)(2,1)} %param.7, bf16[16,256,128]{2,1,0:T(8,128)(2,1)} %all-gather.8.cloned.1.call-done), kind=kOutput, calls=%fused_computation.54 | convolution fusion | flops 134742016 | bytes 13631744 | tf_op jit(solution)/shard_map/rac,vra->vrc/dot_general | solution.py:63
  386.9 20.9 %scatter_fusion.7 = f32[16,17,128]{2,0,1:T(8,128)S(1)} fusion(f32[16,17,128]{2,0,1:T(8,128)S(1)} %broadcast.192, s32[256]{0:T(256)S(1)} %bitcast.118, f32[256,16,128]{2,1,0:T(8,128)} %get-tuple-element.215), kind=kCustom, calls=%fused_computation.14 | custom fusion | flops 524288 | bytes 6292480 | tf_op jit(solution)/shard_map/scatter-add | solution.py:69
  408.5 6.0 %all-to-all-start.6 = ((f32[16,8,2,128]{3,0,2,1:T(8,128)}), f32[16,8,2,128]{3,0,2,1:T(8,128)S(1)}, u32[]{:S(2)}, u32[]{:S(2)}) async-start(f32[16,8,2,128]{3,0,2,1:T(8,128)} %bitcast.34), calls=%async_computation.8 | async-start | bytes 262144 | tf_op jit(solution)/shard_map/all_to_all | solution.py:72
  414.7 2.3 pad_maximum_fusion.2
  417.1 3.0 gather_fusion.5
  420.1 9.5 %fusion.20 = f32[16,256,128]{2,0,1:T(8,128)} fusion(bf16[256,1,128,128]{3,2,1,0:T(8,128)(2,1)} %param.7, bf16[256,16,128]{2,1,0:T(8,128)(2,1)} %gather_fusion.5), kind=kOutput, calls=%fused_computation.38 | convolution fusion | flops 134217728 | bytes 11534336 | tf_op jit(solution)/shard_map/rac,vrc->vra/dot_general | solution.py:62
  429.6 31.4 %scatter_fusion.6 = f32[16,256,128]{2,0,1:T(8,128)} fusion(f32[16,256,128]{2,0,1:T(8,128)} %fusion.20, s32[256]{0:T(256)S(1)} %bitcast.114, f32[256,16,128]{2,1,0:T(8,128)} %get-tuple-element.214), kind=kCustom, calls=%fused_computation.13 | custom fusion | flops 524288 | bytes 6292480 | tf_op jit(solution)/shard_map/scatter-add | solution.py:65
  461.1 2.5 scatter_fusion.8
  463.7 3.1 fusion.28
  466.8 3.6 copy.45
  470.5 31.5 %reduce-scatter.8.cloned.1.call-done = f32[4,256,128]{2,1,0:T(8,128)} async-done(((f32[16,256,128]{2,1,0:T(8,128)}), f32[4,256,128]{2,1,0:T(8,128)}) %reduce-scatter.8.cloned.1.call-update) | async-done | bytes 524304 | tf_op jit(solution)/shard_map/reduce_scatter | solution.py:87
  502.0 1.3 multiply_reduce_fusion
  503.4 21.3 %psum.31 = f32[4]{0:T(128)S(1)} all-reduce(f32[4]{0:T(128)S(1)} %multiply_reduce_fusion), channel_id=1, replica_groups=mesh['curve'=8,'band'=4] {'curve'}, use_global_device_ids=true, to_apply=%region_23.24 | all-reduce | flops 4 | bytes 32 | tf_op jit(solution)/shard_map/psum | solution.py:108
  524.7 1.2 while.20
  525.9 2.1 multiply_add_fusion
  (68 shorter events, 4.3 us)
Async XLA Ops:
  6.5 113.7 %copy-start = (bf16[64,128,128]{2,1,0:T(8,128)(2,1)S(1)}, bf16[64,128,128]{2,1,0:T(8,128)(2,1)}, u32[]{:S(2)}) copy-start(bf16[64,128,128]{2,1,0:T(8,128)(2,1)} %param.8) | copy-start | bytes 6291460
  6.5 21.8 %all-gather.4.cloned.1.call-start = ((), (), s32[]{:S(2)}) async-start(), calls=%async_computation.10 | async-start | bytes 1310720 | tf_op jit(solution)/shard_map/all_gather | solution.py:86
  13.6 13.8 %all-to-all-start = ((s32[8,1,2]{2,1,0:T(1,128)}), s32[8,1,2]{2,1,0:T(1,128)S(1)}, u32[]{:S(2)}, u32[]{:S(2)}) async-start(s32[8,1,2]{2,1,0:T(1,128)} %bitcast.7), calls=%async_computation | async-start | bytes 8192 | tf_op jit(solution)/shard_map/all_to_all | solution.py:46
  31.4 35.1 %all-to-all-start.1 = ((bf16[16,8,2,128]{3,0,2,1:T(8,128)(2,1)}), bf16[16,8,2,128]{3,0,2,1:T(8,128)(2,1)S(1)}, u32[]{:S(2)}, u32[]{:S(2)}) async-start(bf16[16,8,2,128]{3,0,2,1:T(8,128)(2,1)} %bitcast.9), calls=%async_computation.1 | async-start | bytes 131072 | tf_op jit(solution)/shard_map/all_to_all | solution.py:58
  66.6 51.1 %all-to-all-start.2 = ((f32[16,8,2,128]{3,0,2,1:T(8,128)}), f32[16,8,2,128]{3,0,2,1:T(8,128)S(1)}, u32[]{:S(2)}, u32[]{:S(2)}) async-start(f32[16,8,2,128]{3,0,2,1:T(8,128)} %bitcast.16), calls=%async_computation.2 | async-start | bytes 262144 | tf_op jit(solution)/shard_map/all_to_all | solution.py:72
  72.6 86.2 %reduce-scatter.4.cloned.1.call-start = ((), (), s32[]{:S(2)}) async-start(), calls=%async_computation.11 | async-start | bytes 2621440 | tf_op jit(solution)/shard_map/reduce_scatter | solution.py:87
  126.9 31.8 %copy-start.2 = (f32[4,256,128]{2,1,0:T(8,128)S(1)}, f32[4,256,128]{2,1,0:T(8,128)}, u32[]{:S(2)}) copy-start(f32[4,256,128]{2,1,0:T(8,128)} %param.6) | copy-start | bytes 1572868
  127.0 69.5 %all-gather.6.cloned.1.call-start = ((), (), s32[]{:S(2)}) async-start(), calls=%async_computation.12 | async-start | bytes 1310720 | tf_op jit(solution)/shard_map/all_gather | solution.py:86
  201.7 35.1 %all-to-all-start.3 = ((bf16[16,8,2,128]{3,0,2,1:T(8,128)(2,1)}), bf16[16,8,2,128]{3,0,2,1:T(8,128)(2,1)S(1)}, u32[]{:S(2)}, u32[]{:S(2)}) async-start(bf16[16,8,2,128]{3,0,2,1:T(8,128)(2,1)} %bitcast.21), calls=%async_computation.4 | async-start | bytes 131072 | tf_op jit(solution)/shard_map/all_to_all | solution.py:58
  236.9 52.4 %all-to-all-start.4 = ((f32[16,8,2,128]{3,0,2,1:T(8,128)}), f32[16,8,2,128]{3,0,2,1:T(8,128)S(1)}, u32[]{:S(2)}, u32[]{:S(2)}) async-start(f32[16,8,2,128]{3,0,2,1:T(8,128)} %bitcast.25), calls=%async_computation.5 | async-start | bytes 262144 | tf_op jit(solution)/shard_map/all_to_all | solution.py:72
  242.9 87.5 %reduce-scatter.6.cloned.1.call-start = ((), (), s32[]{:S(2)}) async-start(), calls=%async_computation.13 | async-start | bytes 2621440 | tf_op jit(solution)/shard_map/reduce_scatter | solution.py:87
  298.6 69.5 %all-gather.8.cloned.1.call-start = ((), (), s32[]{:S(2)}) async-start(), calls=%async_computation.14 | async-start | bytes 1310720 | tf_op jit(solution)/shard_map/all_gather | solution.py:86
  373.4 35.1 %all-to-all-start.5 = ((bf16[16,8,2,128]{3,0,2,1:T(8,128)(2,1)}), bf16[16,8,2,128]{3,0,2,1:T(8,128)(2,1)S(1)}, u32[]{:S(2)}, u32[]{:S(2)}) async-start(bf16[16,8,2,128]{3,0,2,1:T(8,128)(2,1)} %bitcast.30), calls=%async_computation.7 | async-start | bytes 131072 | tf_op jit(solution)/shard_map/all_to_all | solution.py:58
  408.5 52.6 %all-to-all-start.6 = ((f32[16,8,2,128]{3,0,2,1:T(8,128)}), f32[16,8,2,128]{3,0,2,1:T(8,128)S(1)}, u32[]{:S(2)}, u32[]{:S(2)}) async-start(f32[16,8,2,128]{3,0,2,1:T(8,128)} %bitcast.34), calls=%async_computation.8 | async-start | bytes 262144 | tf_op jit(solution)/shard_map/all_to_all | solution.py:72
  414.5 87.5 %reduce-scatter.8.cloned.1.call-start = ((), (), s32[]{:S(2)}) async-start(), calls=%async_computation.15 | async-start | bytes 2621440 | tf_op jit(solution)/shard_map/reduce_scatter | solution.py:87
  470.4 31.6 %copy-start.1 = (f32[4,256,128]{2,1,0:T(8,128)S(1)}, f32[4,256,128]{2,1,0:T(8,128)}, u32[]{:S(2)}) copy-start(f32[4,256,128]{2,1,0:T(8,128)} %reduce-scatter.6.cloned.1.call-done) | copy-start | bytes 1572868
Sparse Core Ops, SparseCore 0:
  8.9 19.4 all-gather.3
  127.1 31.6 reduce-scatter.3
  183.4 12.9 all-gather.5
  298.7 31.6 reduce-scatter.5
  355.0 12.9 all-gather.7
  470.6 31.3 reduce-scatter.7
where the time goes:
time: 539 us; the launch traced here: 535 us
  other arithmetic  186 us (35%)
  waiting for transfers between devices  128 us (24%)
  blocking collectives  64 us (12%)
  matrix products  61.8 us (11%)
  starting transfers between devices  42.3 us (8%)
  local copies, waits for them, and re-layouts  38.1 us (7%)
  between operations  13.6 us (3%)
    reduce_scatter x3, waiting for transfers between devices, operate(): lax.psum_scatter(local_product(whole, blocks, diag_blocks, plan), 'band',...  95 us
    scatter-add x3, other arithmetic, local_product(): result = result.at[:, target, :].add(kept)  94.3 us
    scatter-add x3, other arithmetic, local_product(): outgoing = jnp.zeros((vectors, groups * CAP + 1, node_count), jnp.float32...  62.8 us
    dot_general x3, matrix products, local_product(): jnp.einsum('rac,vrc->vra', stored, gathered, preferred_element_type=jnp.f...  28.5 us
    all_gather x3, waiting for transfers between devices, operate(): whole = lax.all_gather(vector, 'band', axis=0, tiled=True)  27 us
    dot_general x3, matrix products, local_product(): jnp.einsum('rac,vra->vrc', stored, whole, preferred_element_type=jnp.floa...  24 us
    psum x1, blocking collectives, body(): lax.psum(jnp.sum(second * image_second, axis=(1, 2)), 'curve')  21.3 us
    psum x1, blocking collectives, body(): lax.psum((jnp.sum(first * image, axis=(1, 2)), jnp.sum(image * image, axi...  21.3 us
  transfers between devices with their start and end apart: 13, of which 7 were waited for; matrix products, arithmetic and copies ran while one was open for 43% of the time, Pallas kernels for 0%

commit v1 on v0

--- a/solution.py
+++ b/solution.py
@@ -83,7 +83,10 @@
 
 
 def operate(vector, blocks, diag_blocks, plan):
-    whole = lax.all_gather(vector, "band", axis=0, tiled=True)
+    whole = jnp.concatenate(
+        lax.all_to_all(jnp.stack([vector for _ in range(lax.axis_size("band"))], 0), "band", 0, 0),
+        0,
+    )
     product = lax.psum_scatter(
         local_product(whole, blocks, diag_blocks, plan), "band", scatter_dimension=0, tiled=True
     )

time: 539 us -> 552 us (1.024)
  blocking collectives: 64 us -> 97.7 us
  waiting for transfers between devices: 128 us -> 114 us
    all_to_all x0 -> x2, blocking collectives: none -> 33.7 us  [operate(): lax.all_to_all(jnp.stack([vector for _ in range(lax.axis_size('band'))],...]
    all_gather x3 -> x0, waiting for transfers between devices: 27 us -> none  [operate(): whole = lax.all_gather(vector, 'band', axis=0, tiled=True)]
    all_to_all x0 -> x1, waiting for transfers between devices: none -> 14.2 us  [operate(): lax.all_to_all(jnp.stack([vector for _ in range(lax.axis_size('band'))],...]
    all_gather x3 -> x0, local copies, waits for them, and re-layouts: 7.66 us -> none  [operate(): whole = lax.all_gather(vector, 'band', axis=0, tiled=True)]
    all_to_all x3, starting transfers between devices: 16.5 us -> 10.2 us  [local_product(): lax.all_to_all(reply, 'curve', split_axis=1, concat_axis=1, tiled=True)]
  transfers between devices with their start and end apart: 13 -> 11, of which waited for: 7 -> 5; matrix products, arithmetic and copies ran while one was open for 43% -> 42% of each run, Pallas kernels for 0% -> 0%
where the time goes in v1:
time: 552 us; the launch traced here: 548 us
  other arithmetic  183 us (33%)
  waiting for transfers between devices  114 us (21%)
  blocking collectives  97.7 us (18%)
  matrix products  61.4 us (11%)
  starting transfers between devices  39.7 us (7%)
  local copies, waits for them, and re-layouts  37.2 us (7%)
  between operations  13.4 us (2%)
    reduce_scatter x3, waiting for transfers between devices, operate(): lax.psum_scatter(local_product(whole, blocks, diag_blocks, plan), 'band',...  94.6 us
    scatter-add x3, other arithmetic, local_product(): result = result.at[:, target, :].add(kept)  94.3 us
    scatter-add x3, other arithmetic, local_product(): outgoing = jnp.zeros((vectors, groups * CAP + 1, node_count), jnp.float32...  62.8 us
    all_to_all x2, blocking collectives, operate(): lax.all_to_all(jnp.stack([vector for _ in range(lax.axis_size('band'))],...  33.7 us
    dot_general x3, matrix products, local_product(): jnp.einsum('rac,vrc->vra', stored, gathered, preferred_element_type=jnp.f...  28.5 us
    dot_general x3, matrix products, local_product(): jnp.einsum('rac,vra->vrc', stored, whole, preferred_element_type=jnp.floa...  23.7 us
    psum x1, blocking collectives, body(): lax.psum((jnp.sum(first * image, axis=(1, 2)), jnp.sum(image * image, axi...  21.4 us
    psum x1, blocking collectives, body(): lax.psum(jnp.sum(second * image_second, axis=(1, 2)), 'curve')  21.3 us
  transfers between devices with their start and end apart: 11, of which 5 were waited for; matrix products, arithmetic and copies ran while one was open for 42% of the time, Pallas kernels for 0%

profile of v1, /device:TPU:0, one launch (start us, length us, event | category | flops | bytes accessed | tf_op | source)
XLA Modules:
  0.0 547.9 jit_solution(13934584730631738343)
XLA Ops:
  6.5 0.8 compare_select_fusion
  7.4 0.7 and_select_fusion.3
  8.1 0.7 fusion.44
  9.7 1.4 scatter_custom_fusion
  11.8 7.3 %all-to-all-start.1 = ((s32[8,1,2]{2,1,0:T(1,128)}), s32[8,1,2]{2,1,0:T(1,128)S(1)}, u32[]{:S(2)}, u32[]{:S(2)}) async-start(s32[8,1,2]{2,1,0:T(1,128)} %bitcast.8), calls=%async_computation.1 | async-start | bytes 8192 | tf_op jit(solution)/shard_map/all_to_all | solution.py:46
  19.1 1.1 convert_element_type.21
  20.4 5.1 all-to-all-done.1
  25.5 1.3 stack.6
  26.8 4.2 all-to-all-start
  31.4 14.2 %all-to-all-done = bf16[4,4,256,128]{3,1,2,0:T(4,128)(2,1)} async-done(((bf16[4,4,256,128]{3,1,2,0:T(4,128)(2,1)}), bf16[4,4,256,128]{3,1,2,0:T(4,128)(2,1)}, u32[]{:S(2)}, u32[]{:S(2)}) %all-to-all-start) | async-done | bytes 1048608 | tf_op jit(solution)/shard_map/all_to_all | solution.py:87
  45.6 1.6 copy.18
  47.2 1.2 gather_fusion
  48.4 3.3 all-to-all-start.2
  51.7 7.7 %broadcast_select_fusion.6 = (f32[256,16,128]{2,1,0:T(8,128)}, f32[256,16,128]{2,1,0:T(8,128)}) fusion(pred[256]{0:T(512)(128)(4,1)S(1)} %fusion.43, bf16[16,256,128]{2,0,1:T(8,128)(2,1)S(1)} %bitcast.113, bf16[256,1,128,128]{3,2,1,0:T(8,128)(2,1)} %param.7), kind=kOutput, calls=%fused_computation.56 | convolution fusion | flops 134742016 | bytes 13631744 | tf_op jit(solution)/shard_map/rac,vra->vrc/dot_general | solution.py:63
  59.4 20.9 %scatter_fusion.1 = f32[16,17,128]{2,0,1:T(8,128)S(1)} fusion(f32[16,17,128]{2,0,1:T(8,128)S(1)} %broadcast.198.clone, s32[256]{0:T(256)S(1)} %bitcast.134, f32[256,16,128]{2,1,0:T(8,128)} %get-tuple-element.211), kind=kCustom, calls=%fused_computation.8 | custom fusion | flops 524288 | bytes 6292480 | tf_op jit(solution)/shard_map/scatter-add | solution.py:69
  81.0 5.9 %all-to-all-start.3 = ((f32[16,8,2,128]{3,0,2,1:T(8,128)}), f32[16,8,2,128]{3,0,2,1:T(8,128)S(1)}, u32[]{:S(2)}, u32[]{:S(2)}) async-start(f32[16,8,2,128]{3,0,2,1:T(8,128)} %bitcast.17), calls=%async_computation.3 | async-start | bytes 262144 | tf_op jit(solution)/shard_map/all_to_all | solution.py:72
  87.0 1.1 pad_maximum_fusion
  88.1 3.0 gather_fusion.1
  91.1 9.5 %fusion.14 = f32[16,256,128]{2,0,1:T(8,128)} fusion(bf16[256,1,128,128]{3,2,1,0:T(8,128)(2,1)} %param.7, bf16[256,16,128]{2,1,0:T(8,128)(2,1)} %gather_fusion.1), kind=kOutput, calls=%fused_computation.36 | convolution fusion | flops 134217728 | bytes 11534336 | tf_op jit(solution)/shard_map/rac,vrc->vra/dot_general | solution.py:62
  100.6 31.4 %scatter_fusion = f32[16,256,128]{2,0,1:T(8,128)} fusion(f32[16,256,128]{2,0,1:T(8,128)} %fusion.14, s32[256]{0:T(256)S(1)} %bitcast.130, f32[256,16,128]{2,1,0:T(8,128)} %get-tuple-element.210), kind=kCustom, calls=%fused_computation.7 | custom fusion | flops 524288 | bytes 6292480 | tf_op jit(solution)/shard_map/scatter-add | solution.py:65
  132.1 2.5 scatter_fusion.2
  134.7 3.0 fusion.24
  137.7 3.6 copy.20
  141.3 31.6 %reduce-scatter.4.cloned.1.call-done = f32[4,256,128]{2,1,0:T(8,128)} async-done(((f32[16,256,128]{2,1,0:T(8,128)}), f32[4,256,128]{2,1,0:T(8,128)}) %reduce-scatter.4.cloned.1.call-update) | async-done | bytes 524304 | tf_op jit(solution)/shard_map/reduce_scatter | solution.py:90
  173.0 1.3 multiply_reduce_fusion.3
  174.2 21.3 %psum.28 = f32[4]{0:T(128)S(1)} all-reduce(f32[4]{0:T(128)S(1)} %multiply_reduce_fusion.3), channel_id=1, replica_groups=mesh['curve'=8,'band'=4] {'curve'}, use_global_device_ids=true, to_apply=%region_9.10 | all-reduce | flops 4 | bytes 32 | tf_op jit(solution)/shard_map/psum | solution.py:99
  195.6 1.2 fusion.48
  197.3 16.9 %all_to_all.54 = bf16[4,4,256,128]{3,1,2,0:T(4,128)(2,1)S(1)} all-to-all(bf16[4,4,256,128]{3,1,2,0:T(4,128)(2,1)S(1)} %stack.7), channel_id=1, replica_groups=mesh['curve'=8,'band'=4] {'band'}, dimensions={0} | all-to-all | bytes 2097152 | tf_op jit(solution)/shard_map/all_to_all | solution.py:87
  214.1 1.3 copy.22
  215.5 2.4 gather_fusion.2
  217.9 3.5 all-to-all-start.5
  221.4 8.0 %broadcast_select_fusion.5 = (f32[256,16,128]{2,1,0:T(8,128)}, f32[256,16,128]{2,1,0:T(8,128)}) fusion(pred[256]{0:T(512)(128)(4,1)S(1)} %fusion.43, bf16[16,256,128]{2,0,1:T(8,128)(2,1)} %bitcast.117, bf16[256,1,128,128]{3,2,1,0:T(8,128)(2,1)} %param.7), kind=kOutput, calls=%fused_computation.55 | convolution fusion | flops 134742016 | bytes 13631744 | tf_op jit(solution)/shard_map/rac,vra->vrc/dot_general | solution.py:63
  229.4 20.9 %scatter_fusion.4 = f32[16,17,128]{2,0,1:T(8,128)S(1)} fusion(f32[16,17,128]{2,0,1:T(8,128)S(1)} %broadcast.198.clone.1, s32[256]{0:T(256)S(1)} %bitcast.135, f32[256,16,128]{2,1,0:T(8,128)} %get-tuple-element.213), kind=kCustom, calls=%fused_computation.11 | custom fusion | flops 524288 | bytes 6292480 | tf_op jit(solution)/shard_map/scatter-add | solution.py:69
  251.0 5.8 %all-to-all-start.6 = ((f32[16,8,2,128]{3,0,2,1:T(8,128)}), f32[16,8,2,128]{3,0,2,1:T(8,128)S(1)}, u32[]{:S(2)}, u32[]{:S(2)}) async-start(f32[16,8,2,128]{3,0,2,1:T(8,128)} %bitcast.27), calls=%async_computation.7 | async-start | bytes 262144 | tf_op jit(solution)/shard_map/all_to_all | solution.py:72
  256.8 2.3 pad_maximum_fusion.1
  259.2 3.0 gather_fusion.3
  262.2 9.5 %fusion.17 = f32[16,256,128]{2,0,1:T(8,128)} fusion(bf16[256,1,128,128]{3,2,1,0:T(8,128)(2,1)} %param.7, bf16[256,16,128]{2,1,0:T(8,128)(2,1)} %gather_fusion.3), kind=kOutput, calls=%fused_computation.37 | convolution fusion | flops 134217728 | bytes 11534336 | tf_op jit(solution)/shard_map/rac,vrc->vra/dot_general | solution.py:62
  271.7 31.4 %scatter_fusion.3 = f32[16,256,128]{2,0,1:T(8,128)} fusion(f32[16,256,128]{2,0,1:T(8,128)} %fusion.17, s32[256]{0:T(256)S(1)} %bitcast.131, f32[256,16,128]{2,1,0:T(8,128)} %get-tuple-element.212), kind=kCustom, calls=%fused_computation.10 | custom fusion | flops 524288 | bytes 6292480 | tf_op jit(solution)/shard_map/scatter-add | solution.py:65
  303.2 2.5 scatter_fusion.5
  305.8 3.1 fusion.26
  308.9 3.6 copy.23
  312.5 31.6 %reduce-scatter.6.cloned.1.call-done = f32[4,256,128]{2,1,0:T(8,128)} async-done(((f32[16,256,128]{2,1,0:T(8,128)}), f32[4,256,128]{2,1,0:T(8,128)}) %reduce-scatter.6.cloned.1.call-update) | async-done | bytes 524304 | tf_op jit(solution)/shard_map/reduce_scatter | solution.py:90
  344.2 1.2 multiply_reduce_fusion.1
  345.4 21.4 %all-reduce = (f32[4]{0:T(128)S(1)}, f32[4]{0:T(128)S(1)}) all-reduce(f32[4]{0:T(128)S(1)} %get-tuple-element.175, f32[4]{0:T(128)S(1)} %get-tuple-element.174), channel_id=1, replica_groups=mesh['curve'=8,'band'=4] {'curve'}, use_global_device_ids=true, to_apply=%region_15.16 | all-reduce | flops 8 | bytes 64 | tf_op jit(solution)/shard_map/psum | solution.py:103
  366.8 1.2 fusion.47
  368.5 16.9 %all_to_all.55 = bf16[4,4,256,128]{3,1,2,0:T(4,128)(2,1)S(1)} all-to-all(bf16[4,4,256,128]{3,1,2,0:T(4,128)(2,1)S(1)} %stack.8), channel_id=1, replica_groups=mesh['curve'=8,'band'=4] {'band'}, dimensions={0} | all-to-all | bytes 2097152 | tf_op jit(solution)/shard_map/all_to_all | solution.py:87
  385.3 1.3 copy.25
  386.7 2.4 gather_fusion.4
  389.1 3.3 all-to-all-start.8
  392.4 8.0 %broadcast_select_fusion.4 = (f32[256,16,128]{2,1,0:T(8,128)}, f32[256,16,128]{2,1,0:T(8,128)}) fusion(pred[256]{0:T(512)(128)(4,1)S(1)} %fusion.43, bf16[16,256,128]{2,0,1:T(8,128)(2,1)} %bitcast.109, bf16[256,1,128,128]{3,2,1,0:T(8,128)(2,1)} %param.7), kind=kOutput, calls=%fused_computation.54 | convolution fusion | flops 134742016 | bytes 13631744 | tf_op jit(solution)/shard_map/rac,vra->vrc/dot_general | solution.py:63
  400.4 20.9 %scatter_fusion.7 = f32[16,17,128]{2,0,1:T(8,128)S(1)} fusion(f32[16,17,128]{2,0,1:T(8,128)S(1)} %broadcast.198, s32[256]{0:T(256)S(1)} %bitcast.136, f32[256,16,128]{2,1,0:T(8,128)} %get-tuple-element.215), kind=kCustom, calls=%fused_computation.14 | custom fusion | flops 524288 | bytes 6292480 | tf_op jit(solution)/shard_map/scatter-add | solution.py:69
  422.0 5.9 %all-to-all-start.9 = ((f32[16,8,2,128]{3,0,2,1:T(8,128)}), f32[16,8,2,128]{3,0,2,1:T(8,128)S(1)}, u32[]{:S(2)}, u32[]{:S(2)}) async-start(f32[16,8,2,128]{3,0,2,1:T(8,128)} %bitcast.37), calls=%async_computation.11 | async-start | bytes 262144 | tf_op jit(solution)/shard_map/all_to_all | solution.py:72
  428.2 2.3 pad_maximum_fusion.2
  430.6 3.0 gather_fusion.5
  433.6 9.5 %fusion.20 = f32[16,256,128]{2,0,1:T(8,128)} fusion(bf16[256,1,128,128]{3,2,1,0:T(8,128)(2,1)} %param.7, bf16[256,16,128]{2,1,0:T(8,128)(2,1)} %gather_fusion.5), kind=kOutput, calls=%fused_computation.38 | convolution fusion | flops 134217728 | bytes 11534336 | tf_op jit(solution)/shard_map/rac,vrc->vra/dot_general | solution.py:62
  443.1 31.4 %scatter_fusion.6 = f32[16,256,128]{2,0,1:T(8,128)} fusion(f32[16,256,128]{2,0,1:T(8,128)} %fusion.20, s32[256]{0:T(256)S(1)} %bitcast.132, f32[256,16,128]{2,1,0:T(8,128)} %get-tuple-element.214), kind=kCustom, calls=%fused_computation.13 | custom fusion | flops 524288 | bytes 6292480 | tf_op jit(solution)/shard_map/scatter-add | solution.py:65
  474.6 2.5 scatter_fusion.8
  477.2 3.1 fusion.28
  480.3 3.6 copy.26
  484.0 31.4 %reduce-scatter.8.cloned.1.call-done = f32[4,256,128]{2,1,0:T(8,128)} async-done(((f32[16,256,128]{2,1,0:T(8,128)}), f32[4,256,128]{2,1,0:T(8,128)}) %reduce-scatter.8.cloned.1.call-update) | async-done | bytes 524304 | tf_op jit(solution)/shard_map/reduce_scatter | solution.py:90
  515.4 1.3 multiply_reduce_fusion
  516.7 21.3 %psum.31 = f32[4]{0:T(128)S(1)} all-reduce(f32[4]{0:T(128)S(1)} %multiply_reduce_fusion), channel_id=1, replica_groups=mesh['curve'=8,'band'=4] {'curve'}, use_global_device_ids=true, to_apply=%region_23.24 | all-reduce | flops 4 | bytes 32 | tf_op jit(solution)/shard_map/psum | solution.py:111
  538.0 1.2 while.20
  539.3 2.1 multiply_add_fusion
  (71 shorter events, 6.0 us)
Async XLA Ops:
  6.5 128.1 %copy-start = (bf16[64,128,128]{2,1,0:T(8,128)(2,1)S(1)}, bf16[64,128,128]{2,1,0:T(8,128)(2,1)}, u32[]{:S(2)}) copy-start(bf16[64,128,128]{2,1,0:T(8,128)(2,1)} %param.8) | copy-start | bytes 6291460
  11.8 13.7 %all-to-all-start.1 = ((s32[8,1,2]{2,1,0:T(1,128)}), s32[8,1,2]{2,1,0:T(1,128)S(1)}, u32[]{:S(2)}, u32[]{:S(2)}) async-start(s32[8,1,2]{2,1,0:T(1,128)} %bitcast.8), calls=%async_computation.1 | async-start | bytes 8192 | tf_op jit(solution)/shard_map/all_to_all | solution.py:46
  20.2 10.9 %copy-start.3 = (s32[256,1]{0,1:T(1,128)S(1)}, s32[256,1]{0,1:T(1,128)}, u32[]{:S(2)}) copy-start(s32[256,1]{0,1:T(1,128)} %param.9) | copy-start | bytes 3076
  26.8 18.7 %all-to-all-start = ((bf16[4,4,256,128]{3,1,2,0:T(4,128)(2,1)}), bf16[4,4,256,128]{3,1,2,0:T(4,128)(2,1)}, u32[]{:S(2)}, u32[]{:S(2)}) async-start(bf16[4,4,256,128]{3,1,2,0:T(4,128)(2,1)} %stack.6), calls=%async_computation | async-start | bytes 2097152 | tf_op jit(solution)/shard_map/all_to_all | solution.py:87
  48.4 32.6 %all-to-all-start.2 = ((bf16[16,8,2,128]{3,0,2,1:T(8,128)(2,1)}), bf16[16,8,2,128]{3,0,2,1:T(8,128)(2,1)S(1)}, u32[]{:S(2)}, u32[]{:S(2)}) async-start(bf16[16,8,2,128]{3,0,2,1:T(8,128)(2,1)} %bitcast.10), calls=%async_computation.2 | async-start | bytes 131072 | tf_op jit(solution)/shard_map/all_to_all | solution.py:58
  81.0 51.0 %all-to-all-start.3 = ((f32[16,8,2,128]{3,0,2,1:T(8,128)}), f32[16,8,2,128]{3,0,2,1:T(8,128)S(1)}, u32[]{:S(2)}, u32[]{:S(2)}) async-start(f32[16,8,2,128]{3,0,2,1:T(8,128)} %bitcast.17), calls=%async_computation.3 | async-start | bytes 262144 | tf_op jit(solution)/shard_map/all_to_all | solution.py:72
  86.9 86.1 %reduce-scatter.4.cloned.1.call-start = ((), (), s32[]{:S(2)}) async-start(), calls=%async_computation.13 | async-start | bytes 2621440 | tf_op jit(solution)/shard_map/reduce_scatter | solution.py:90
  141.3 31.7 %copy-start.2 = (f32[4,256,128]{2,1,0:T(8,128)S(1)}, f32[4,256,128]{2,1,0:T(8,128)}, u32[]{:S(2)}) copy-start(f32[4,256,128]{2,1,0:T(8,128)} %param.6) | copy-start | bytes 1572868
  217.9 33.1 %all-to-all-start.5 = ((bf16[16,8,2,128]{3,0,2,1:T(8,128)(2,1)}), bf16[16,8,2,128]{3,0,2,1:T(8,128)(2,1)S(1)}, u32[]{:S(2)}, u32[]{:S(2)}) async-start(bf16[16,8,2,128]{3,0,2,1:T(8,128)(2,1)} %bitcast.23), calls=%async_computation.6 | async-start | bytes 131072 | tf_op jit(solution)/shard_map/all_to_all | solution.py:58
  251.0 52.1 %all-to-all-start.6 = ((f32[16,8,2,128]{3,0,2,1:T(8,128)}), f32[16,8,2,128]{3,0,2,1:T(8,128)S(1)}, u32[]{:S(2)}, u32[]{:S(2)}) async-start(f32[16,8,2,128]{3,0,2,1:T(8,128)} %bitcast.27), calls=%async_computation.7 | async-start | bytes 262144 | tf_op jit(solution)/shard_map/all_to_all | solution.py:72
  256.8 87.4 %reduce-scatter.6.cloned.1.call-start = ((), (), s32[]{:S(2)}) async-start(), calls=%async_computation.14 | async-start | bytes 2621440 | tf_op jit(solution)/shard_map/reduce_scatter | solution.py:90
  389.1 33.0 %all-to-all-start.8 = ((bf16[16,8,2,128]{3,0,2,1:T(8,128)(2,1)}), bf16[16,8,2,128]{3,0,2,1:T(8,128)(2,1)S(1)}, u32[]{:S(2)}, u32[]{:S(2)}) async-start(bf16[16,8,2,128]{3,0,2,1:T(8,128)(2,1)} %bitcast.33), calls=%async_computation.10 | async-start | bytes 131072 | tf_op jit(solution)/shard_map/all_to_all | solution.py:58
  422.0 52.5 %all-to-all-start.9 = ((f32[16,8,2,128]{3,0,2,1:T(8,128)}), f32[16,8,2,128]{3,0,2,1:T(8,128)S(1)}, u32[]{:S(2)}, u32[]{:S(2)}) async-start(f32[16,8,2,128]{3,0,2,1:T(8,128)} %bitcast.37), calls=%async_computation.11 | async-start | bytes 262144 | tf_op jit(solution)/shard_map/all_to_all | solution.py:72
  428.0 87.4 %reduce-scatter.8.cloned.1.call-start = ((), (), s32[]{:S(2)}) async-start(), calls=%async_computation.15 | async-start | bytes 2621440 | tf_op jit(solution)/shard_map/reduce_scatter | solution.py:90
  483.9 31.4 %copy-start.1 = (f32[4,256,128]{2,1,0:T(8,128)S(1)}, f32[4,256,128]{2,1,0:T(8,128)}, u32[]{:S(2)}) copy-start(f32[4,256,128]{2,1,0:T(8,128)} %reduce-scatter.6.cloned.1.call-done) | copy-start | bytes 1572868
Sparse Core Ops, SparseCore 0:
  141.5 31.4 reduce-scatter.3
  312.7 31.4 reduce-scatter.5
  484.1 31.2 reduce-scatter.7
